TPU v7x, 256 devices: a whole 4x4x8 slice. The times are simulated.
256 devices in a mesh: row: 16 (over z, core), col: 16 (over y, x).
Axes of the slice: x: 4, y: 4, z: 8, core: 2. Of those that a mesh axis runs over, the one named last changes fastest.
Arguments:
- front_blocks: bfloat16 [64, 5, 512, 512], P('row'), may hold values from -0.125 to 0.125
- block_cols: int32 [64, 5], P('row'), may hold values from 0 to 63, as said below
- samples: bfloat16 [32768, 1024], P('row', 'col'), may hold values from -6 to 6
- sketch_matrix: bfloat16 [1024, 256], replicated, may hold values from -0.1875 to 0.1875
Outputs:
- leaf_bases: bfloat16 [32768, 256], P('row')
- top_transfers: bfloat16 [1024, 256], P('row')
Inputs may be any that keep to these rules, and one draw needn't show every extreme that they name: `block_cols`: each row lists 5 different block columns; the first is the row's own index, the second lies in the other half of the 64 block columns (its index differs in the highest bit).
All inputs are finite; a program needn't handle non-finite values.
Results may differ from a plain program's by a relative error of at most 0.035.
Values may be sent and summed in bfloat16 or wider, within the bound.
No kernel may reach another device: no remote copies, remote signals or barrier semaphores. Data moves between devices by JAX's collectives and lax.ppermute only.
A program may use at most 128 MiB of HBM per device.

v0:
```python
import math
import jax
import jax.numpy as jnp
from jax import lax
from jax.sharding import PartitionSpec as P


def partner_2(value, axis, stride):
    mask = 2**stride
    pairs = [(source, source ^ mask) for source in range(lax.axis_size(axis))]
    return lax.ppermute(value, axis, pairs)


def cholqr(sketch):
    highest = lax.Precision.HIGHEST
    gram_matrix = jnp.dot(sketch.T, sketch, precision=highest)
    low_factor = jnp.linalg.cholesky(gram_matrix)
    identity = jnp.eye(sketch.shape[1], dtype=sketch.dtype)
    low_inverse = jax.scipy.linalg.solve_triangular(low_factor, identity, lower=True)
    ortho_basis = jnp.dot(sketch, low_inverse.T, precision=highest)
    return (ortho_basis * math.sqrt(sketch.shape[0])).astype(jnp.bfloat16)


def off_products(all_sketched, front_blocks, block_cols, leaf_ids, top_level):
    leaf_total = all_sketched.shape[0] // front_blocks.shape[2]
    gathered_blocks = all_sketched.reshape(
        leaf_total, front_blocks.shape[2], all_sketched.shape[1]
    )[block_cols]
    products = jnp.einsum(
        "nkab,nkbc->nkac", front_blocks, gathered_blocks, preferred_element_type=jnp.float32
    )
    level_ids = jnp.arange(top_level, dtype=jnp.int32)
    outside = (
        jnp.right_shift(leaf_ids[:, None, None], level_ids[None, :, None])
        != jnp.right_shift(block_cols[:, None, :], level_ids[None, :, None])
    ).astype(jnp.float32)
    return jnp.einsum("nlk,nkac->nlac", outside, products, precision=lax.Precision.HIGHEST).astype(
        jnp.bfloat16
    )


def shards(front_blocks, block_cols, samples, sketch_matrix):
    leaf_dev = front_blocks.shape[0]
    leaf_size = front_blocks.shape[2]
    rank_size = sketch_matrix.shape[1]
    cols_dev = samples.shape[1]
    size_rows = lax.axis_size("row")
    row_index = lax.axis_index("row")
    leaf_total = leaf_dev * size_rows
    top_level = leaf_total.bit_length() - 1
    local_levels = leaf_dev.bit_length() - 1
    leaf_ids = row_index * leaf_dev + jnp.arange(leaf_dev, dtype=jnp.int32)
    local_rows = lax.dynamic_slice_in_dim(
        sketch_matrix, lax.axis_index("col") * cols_dev, cols_dev, 0
    )
    partial_sum = jnp.dot(samples, local_rows, preferred_element_type=jnp.float32)
    sketched = lax.psum(partial_sum.astype(jnp.bfloat16), "col")
    all_sketched = lax.all_gather(sketched, "row", axis=0, tiled=True)
    off_samples = off_products(all_sketched, front_blocks, block_cols, leaf_ids, top_level)
    leaf_basis = jax.vmap(cholqr)(off_samples[:, 0].astype(jnp.float32))
    carried = jnp.einsum(
        "nar,nlac->nlrc", leaf_basis, off_samples[:, 1:], preferred_element_type=jnp.float32
    )
    carried = (carried * (1.0 / math.sqrt(leaf_size))).astype(jnp.bfloat16)
    scale_pair = 1.0 / math.sqrt(2 * rank_size)
    transfer = None
    for tree_level in range(1, top_level):
        if carried.shape[0] >= 2:
            node_count = carried.shape[0] // 2
            paired = carried.reshape(node_count, 2, carried.shape[1], rank_size, rank_size)
            stacked = jnp.concatenate([paired[:, 0], paired[:, 1]], axis=2)
        else:
            swap_bit = tree_level - local_levels - 1
            is_left = jnp.right_shift(row_index, swap_bit) % 2 == 0
            partner = partner_2(carried, "row", swap_bit)
            left_part = jnp.where(is_left, carried, partner)
            right_part = jnp.where(is_left, partner, carried)
            stacked = jnp.concatenate([left_part, right_part], axis=2)
        transfer = jax.vmap(cholqr)(stacked[:, 0].astype(jnp.float32))
        if tree_level < top_level - 1:
            moved = jnp.einsum(
                "npr,nlpc->nlrc", transfer, stacked[:, 1:], preferred_element_type=jnp.float32
            )
            carried = (moved * scale_pair).astype(jnp.bfloat16)
    out_rows = 4 * rank_size // size_rows
    offset = row_index % (size_rows // 2) * out_rows
    top_rows = lax.dynamic_slice_in_dim(transfer[0], offset, out_rows, 0)
    return (leaf_basis.reshape(leaf_dev * leaf_size, rank_size), top_rows)


def solution(mesh):
    placed = (P("row", None, None, None), P("row", None), P("row", "col"), P())
    return jax.shard_map(
        shards,
        mesh=mesh,
        in_specs=placed,
        out_specs=(P("row", None), P("row", None)),
        check_vma=False,
    )
```

profile of v0, /device:TPU:1, one launch (start us, length us, event | category | flops | bytes accessed | tf_op | source)
XLA Modules:
  0.0 963.2 jit_solution(16113320740704673089)
XLA Ops:
  8.2 2.4 fusion.2
  10.7 100.7 %all-reduce.5.cloned.1.call-done = bf16[2048,256]{0,1:T(8,128)(2,1)} async-done(((bf16[2048,256]{0,1:T(8,128)(2,1)}), bf16[2048,256]{0,1:T(8,128)(2,1)}) %all-reduce.5.cloned.1.call-update) | async-done | bytes 1048592 | tf_op jit(solution)/shard_map/psum | solution.py:57
  111.8 98.0 %all-gather.2.cloned.1.call-done = bf16[32768,256]{0,1:T(8,128)(2,1)} async-done(((bf16[2048,256]{0,1:T(8,128)(2,1)}), bf16[32768,256]{0,1:T(8,128)(2,1)}) %all-gather.2.cloned.1.call-update) | async-done | bytes 16777232 | tf_op jit(solution)/shard_map/all_gather | solution.py:58
  209.8 22.4 %copy.112 = bf16[32768,256]{1,0:T(8,128)(2,1)} copy(bf16[32768,256]{0,1:T(8,128)(2,1)} %all-gather.2.cloned.1.call-done) | data formatting | bytes 33554432 | tf_op jit(solution)/shard_map/reshape | solution.py:26
  232.2 9.9 %gather_fusion = bf16[20,512,256]{2,1,0:T(8,128)(2,1)} fusion(bf16[64,512,256]{2,1,0:T(8,128)(2,1)} %bitcast.432, s32[1024]{0:T(1024)S(1)} %pad_clamp_fusion), kind=kCustom, calls=%fused_computation | custom fusion | bytes 10485840 | tf_op jit(solution)/shard_map/gather | solution.py:26
  242.0 12.5 %convolution_bitcast_fusion = f32[4,5,512,256]{2,3,1,0:T(8,128)} fusion(bf16[4,5,512,256]{3,2,1,0:T(8,128)(2,1)} %bitcast.433, bf16[4,5,512,512]{3,2,1,0:T(8,128)(2,1)} %param.7), kind=kOutput, calls=%fused_computation.17 | convolution fusion | flops 2684354560 | bytes 26214400 | tf_op jit(solution)/shard_map/nkab,nkbc->nkac/dot_general | solution.py:29
  254.6 17.1 %copy.63 = f32[4,5,512,256]{3,1,2,0:T(8,128)} copy(f32[4,5,512,256]{2,3,1,0:T(8,128)} %convolution_bitcast_fusion) | data formatting | bytes 20971520 | tf_op jit(solution)/shard_map/nkab,nkbc->nkac/dot_general | solution.py:29
  271.7 11.9 %convolution_convert_fusion = bf16[4,6,512,256]{3,1,2,0:T(8,128)(2,1)S(1)} fusion(f32[4,5,512,256]{3,1,2,0:T(8,128)} %copy.63, s32[4,5]{1,0:T(4,128)S(1)} %copy-done.11, s32[4,6]{1,0:T(4,128)S(1)} %iota_shift-right-arithmetic_fusion), kind=kOutput, calls=%fused_computation.13 | convolution fusion | flops 191889648 | bytes 16777392 | tf_op jit(solution)/shard_map/nlk,nkac->nlac/dot_general | solution.py:37
  283.6 3.2 copy-done.2
  288.3 9.4 slice.235
  299.7 46.9 %custom-call.47 = f32[4,128,128]{2,1,0:T(8,128)S(1)} custom-call(f32[4,128,128]{2,1,0:T(8,128)S(1)} %cholesky.577), custom_call_target="Cholesky" | custom-call | tf_op jit(solution)/shard_map/vmap(jit(cholesky))/cholesky | solution.py:17
  346.7 39.3 %custom-call.48 = f32[4,1,128,128]{2,3,1,0:T(8,128)S(1)} custom-call(f32[4,1,128,128]{3,2,1,0:T(8,128)S(1)} %select_bitcast_fusion), custom_call_target="InvertDiagBlocksLowerTriangular" | custom-call | tf_op jit(solution)/shard_map/vmap(jit(cholesky))/cholesky | solution.py:17
  389.1 59.6 %custom-call.49 = f32[4,128,128]{2,1,0:T(8,128)S(1)} custom-call(f32[4,128,128]{2,1,0:T(8,128)S(1)} %convolution_subtract_fusion.2), custom_call_target="Cholesky" | custom-call | tf_op jit(solution)/shard_map/vmap(jit(cholesky))/cholesky | solution.py:17
  449.2 5.3 while.10
  449.8 2.1 bitcast_dynamic-update-slice_fusion.16
  452.4 2.1 bitcast_dynamic-update-slice_fusion.16
  454.5 79.4 %custom-call.50 = f32[4,2,128,128]{2,3,1,0:T(8,128)S(1)} custom-call(f32[4,2,128,128]{3,2,1,0:T(8,128)} %bitcast.451), custom_call_target="InvertDiagBlocksLowerTriangular" | custom-call | tf_op jit(solution)/shard_map/vmap(jit(_solve_triangular))/triangular_solve | solution.py:19
  535.8 2.7 multiply_convert_fusion.2
  538.5 5.7 multiply_convert_fusion
  550.6 24.3 %custom-call.51 = f32[2,128,128]{2,1,0:T(8,128)S(1)} custom-call(f32[2,128,128]{2,1,0:T(8,128)} %cholesky.580), custom_call_target="Cholesky" | custom-call | tf_op jit(solution)/shard_map/vmap(jit(cholesky))/cholesky | solution.py:17
  577.1 21.5 %custom-call.52 = f32[2,1,128,128]{2,3,1,0:T(8,128)} custom-call(f32[2,1,128,128]{3,2,1,0:T(8,128)} %select_bitcast_fusion.1), custom_call_target="InvertDiagBlocksLowerTriangular" | custom-call | tf_op jit(solution)/shard_map/vmap(jit(cholesky))/cholesky | solution.py:17
  602.5 24.9 %custom-call.53 = f32[2,128,128]{2,1,0:T(8,128)} custom-call(f32[2,128,128]{2,1,0:T(8,128)} %convolution_subtract_fusion.3), custom_call_target="Cholesky" | custom-call | tf_op jit(solution)/shard_map/vmap(jit(cholesky))/cholesky | solution.py:17
  631.2 8.3 while.11
  632.4 3.0 bitcast_dynamic-update-slice_fusion.17
  636.6 2.9 bitcast_dynamic-update-slice_fusion.17
  639.6 40.9 %custom-call.54 = f32[2,2,128,128]{2,3,1,0:T(8,128)} custom-call(f32[2,2,128,128]{3,2,1,0:T(8,128)} %bitcast.452), custom_call_target="InvertDiagBlocksLowerTriangular" | custom-call | tf_op jit(solution)/shard_map/vmap(jit(_solve_triangular))/triangular_solve | solution.py:19
  686.5 11.7 %custom-call.67 = f32[1,128,128]{2,1,0:T(8,128)S(1)} custom-call(f32[1,128,128]{2,1,0:T(8,128)S(1)} %cholesky.583), custom_call_target="Cholesky" | custom-call | tf_op jit(solution)/shard_map/vmap(jit(cholesky))/cholesky | solution.py:17
  698.3 9.8 %custom-call.68 = f32[1,1,128,128]{2,3,1,0:T(8,128)S(1)} custom-call(f32[1,1,128,128]{3,2,1,0:T(8,128)S(1)} %get-tuple-element.143), custom_call_target="InvertDiagBlocksLowerTriangular" | custom-call | tf_op jit(solution)/shard_map/vmap(jit(cholesky))/cholesky | solution.py:17
  708.6 12.1 %custom-call.69 = f32[1,128,128]{2,1,0:T(8,128)S(1)} custom-call(f32[1,128,128]{2,1,0:T(8,128)S(1)} %fusion.34), custom_call_target="Cholesky" | custom-call | tf_op jit(solution)/shard_map/vmap(jit(cholesky))/cholesky | solution.py:17
  723.5 4.1 while.12
  727.6 19.7 %custom-call.70 = f32[1,2,128,128]{2,3,1,0:T(8,128)S(1)} custom-call(f32[1,2,128,128]{3,2,1,0:T(8,128)S(1)} %bitcast.448), custom_call_target="InvertDiagBlocksLowerTriangular" | custom-call | tf_op jit(solution)/shard_map/vmap(jit(_solve_triangular))/triangular_solve | solution.py:19
  751.4 11.7 %custom-call.71 = f32[1,128,128]{2,1,0:T(8,128)S(1)} custom-call(f32[1,128,128]{2,1,0:T(8,128)S(1)} %cholesky.586), custom_call_target="Cholesky" | custom-call | tf_op jit(solution)/shard_map/vmap(jit(cholesky))/cholesky | solution.py:17
  763.2 9.8 %custom-call.72 = f32[1,1,128,128]{2,3,1,0:T(8,128)S(1)} custom-call(f32[1,1,128,128]{3,2,1,0:T(8,128)S(1)} %get-tuple-element.139), custom_call_target="InvertDiagBlocksLowerTriangular" | custom-call | tf_op jit(solution)/shard_map/vmap(jit(cholesky))/cholesky | solution.py:17
  773.5 11.7 %custom-call.73 = f32[1,128,128]{2,1,0:T(8,128)S(1)} custom-call(f32[1,128,128]{2,1,0:T(8,128)S(1)} %fusion.35), custom_call_target="Cholesky" | custom-call | tf_op jit(solution)/shard_map/vmap(jit(cholesky))/cholesky | solution.py:17
  787.9 4.2 while.13
  792.2 19.7 %custom-call.74 = f32[1,2,128,128]{2,3,1,0:T(8,128)S(1)} custom-call(f32[1,2,128,128]{3,2,1,0:T(8,128)S(1)} %bitcast.449), custom_call_target="InvertDiagBlocksLowerTriangular" | custom-call | tf_op jit(solution)/shard_map/vmap(jit(_solve_triangular))/triangular_solve | solution.py:19
  813.6 7.6 collective-permute-done.1
  821.8 11.7 %custom-call.75 = f32[1,128,128]{2,1,0:T(8,128)S(1)} custom-call(f32[1,128,128]{2,1,0:T(8,128)S(1)} %cholesky.589), custom_call_target="Cholesky" | custom-call | tf_op jit(solution)/shard_map/vmap(jit(cholesky))/cholesky | solution.py:17
  833.5 9.8 %custom-call.76 = f32[1,1,128,128]{2,3,1,0:T(8,128)S(1)} custom-call(f32[1,1,128,128]{3,2,1,0:T(8,128)S(1)} %get-tuple-element.135), custom_call_target="InvertDiagBlocksLowerTriangular" | custom-call | tf_op jit(solution)/shard_map/vmap(jit(cholesky))/cholesky | solution.py:17
  843.8 11.7 %custom-call.77 = f32[1,128,128]{2,1,0:T(8,128)S(1)} custom-call(f32[1,128,128]{2,1,0:T(8,128)S(1)} %fusion.36), custom_call_target="Cholesky" | custom-call | tf_op jit(solution)/shard_map/vmap(jit(cholesky))/cholesky | solution.py:17
  858.3 4.3 while.14
  862.5 19.7 %custom-call.78 = f32[1,2,128,128]{2,3,1,0:T(8,128)S(1)} custom-call(f32[1,2,128,128]{3,2,1,0:T(8,128)S(1)} %bitcast.450), custom_call_target="InvertDiagBlocksLowerTriangular" | custom-call | tf_op jit(solution)/shard_map/vmap(jit(_solve_triangular))/triangular_solve | solution.py:19
  885.6 7.2 collective-permute-done.2
  893.3 11.7 %custom-call.79 = f32[1,128,128]{2,1,0:T(8,128)S(1)} custom-call(f32[1,128,128]{2,1,0:T(8,128)S(1)} %cholesky.592), custom_call_target="Cholesky" | custom-call | tf_op jit(solution)/shard_map/vmap(jit(cholesky))/cholesky | solution.py:17
  905.1 9.8 %custom-call.80 = f32[1,1,128,128]{2,3,1,0:T(8,128)S(1)} custom-call(f32[1,1,128,128]{3,2,1,0:T(8,128)S(1)} %get-tuple-element.131), custom_call_target="InvertDiagBlocksLowerTriangular" | custom-call | tf_op jit(solution)/shard_map/vmap(jit(cholesky))/cholesky | solution.py:17
  915.4 11.7 %custom-call.81 = f32[1,128,128]{2,1,0:T(8,128)S(1)} custom-call(f32[1,128,128]{2,1,0:T(8,128)S(1)} %fusion.37), custom_call_target="Cholesky" | custom-call | tf_op jit(solution)/shard_map/vmap(jit(cholesky))/cholesky | solution.py:17
  929.9 4.4 while.15
  934.3 19.7 %custom-call.82 = f32[1,2,128,128]{2,3,1,0:T(8,128)S(1)} custom-call(f32[1,2,128,128]{3,2,1,0:T(8,128)S(1)} %bitcast.447), custom_call_target="InvertDiagBlocksLowerTriangular" | custom-call | tf_op jit(solution)/shard_map/vmap(jit(_solve_triangular))/triangular_solve | solution.py:19
  (199 shorter events, 72.1 us)
Async XLA Ops:
  7.2 1.1 copy-start
  7.2 104.2 %copy-start.11 = (s32[4,5]{1,0:T(4,128)S(1)}, s32[4,5]{1,0:T(4,128)}, u32[]{:S(2)}) copy-start(s32[4,5]{1,0:T(4,128)} %param.8) | copy-start | bytes 244
  7.2 104.2 %all-reduce.5.cloned.1.call-start = ((), (), s32[]{:S(2)}) async-start(), calls=%async_computation | async-start | bytes 2097152 | tf_op jit(solution)/shard_map/psum | solution.py:57
  10.6 199.2 %all-gather.2.cloned.1.call-start = ((), (), s32[]{:S(2)}) async-start(), calls=%async_computation.1 | async-start | bytes 17825792 | tf_op jit(solution)/shard_map/all_gather | solution.py:58
  111.5 235.1 %copy-start.10 = (pred[128,128]{1,0:T(8,128)(4,1)}, pred[128,128]{1,0:T(8,128)(4,1)S(1)}, u32[]{:S(2)}) copy-start(pred[128,128]{1,0:T(8,128)(4,1)S(1)} %iota_compare_fusion.5) | copy-start | bytes 49156
  111.6 337.3 %copy-start.9 = (pred[256,256]{1,0:T(8,128)(4,1)}, pred[256,256]{1,0:T(8,128)(4,1)S(1)}, u32[]{:S(2)}) copy-start(pred[256,256]{1,0:T(8,128)(4,1)S(1)} %iota_compare_fusion.2) | copy-start | bytes 196612
  111.8 422.2 %copy-start.6 = (f32[128,256]{1,0:T(8,128)}, f32[128,256]{1,0:T(8,128)S(1)}, u32[]{:S(2)}) copy-start(f32[128,256]{1,0:T(8,128)S(1)} %get-tuple-element.125) | copy-start | bytes 393220
  111.8 422.8 %copy-start.8 = (f32[128,256]{1,0:T(8,128)}, f32[128,256]{1,0:T(8,128)S(1)}, u32[]{:S(2)}) copy-start(f32[128,256]{1,0:T(8,128)S(1)} %get-tuple-element.124) | copy-start | bytes 393220
  283.6 3.2 copy-start.2
  288.3 9.4 copy-start.4
  298.7 1.0 copy-start.3
  454.5 84.0 %copy-start.13 = (s32[2,2]{1,0:T(2,128)}, s32[2,2]{1,0:T(2,128)S(1)}, u32[]{:S(2)}) copy-start(s32[2,2]{1,0:T(2,128)S(1)} %get-tuple-element.442) | copy-start | bytes 52
  538.5 5.7 copy-start.12
  549.2 0.8 copy-start.5
  629.0 51.5 %copy-start.7 = (f32[128,256]{1,0:T(8,128)S(1)}, f32[128,256]{1,0:T(8,128)}, u32[]{:S(2)}) copy-start(f32[128,256]{1,0:T(8,128)} %copy-done.6) | copy-start | bytes 393220
  686.0 37.5 %copy-start.14 = (s32[2,2]{1,0:T(2,128)S(1)}, s32[2,2]{1,0:T(2,128)}, u32[]{:S(2)}) copy-start(s32[2,2]{1,0:T(2,128)} %get-tuple-element.443) | copy-start | bytes 52
  749.1 1.8 collective-permute-start
  813.5 7.7 collective-permute-start.1
  883.8 9.0 collective-permute-start.2
  893.3 62.7 %copy-start.1 = (bf16[1024,256]{1,0:T(8,128)(2,1)S(1)}, bf16[1024,256]{1,0:T(8,128)(2,1)}, u32[]{:S(2)}) copy-start(bf16[1024,256]{1,0:T(8,128)(2,1)} %param.10) | copy-start | bytes 1572868
Sparse Core Ops, SparseCore 0:
  11.8 99.4 all-reduce.4
  113.2 96.5 all-gather.1
where the time goes:
time: 972 us; the launch traced here: 963 us
  other arithmetic  563 us (58%)
  waiting for transfers between devices  215 us (22%)
  local copies, waits for them, and re-layouts  101 us (10%)
  matrix products  60.2 us (6%)
  between operations  20.7 us (2%)
    another operation x45, other arithmetic, cholqr(): low_factor = jnp.linalg.cholesky(gram_matrix)  359 us
    another operation x14, other arithmetic, cholqr(): jax.scipy.linalg.solve_triangular(low_factor, identity, lower=True)  201 us
    psum x1, waiting for transfers between devices, shards(): sketched = lax.psum(partial_sum.astype(jnp.bfloat16), 'col')  101 us
    all_gather x1, waiting for transfers between devices, shards(): all_sketched = lax.all_gather(sketched, 'row', axis=0, tiled=True)  98 us
    reshape x1, local copies, waits for them, and re-layouts, off_products(): all_sketched.reshape(leaf_total, front_blocks.shape[2], all_sketched.shap...  22.4 us
  transfers between devices with their start and end apart: 5, of which 5 were waited for; matrix products, arithmetic and copies ran while one was open for 0% of the time, Pallas kernels for 0%

commit v1 on v0

--- a/solution.py
+++ b/solution.py
@@ -1,8 +1,19 @@
+import functools
 import math
 import jax
 import jax.numpy as jnp
 from jax import lax
 from jax.sharding import PartitionSpec as P
+
+
+def _measure_local_data(state, on_dim):
+    outcome_arr = lax.all_to_all(
+        jnp.stack([state for _ in range(lax.axis_size("row"))]), "row", split_axis=0, concat_axis=0
+    )
+    return jnp.concatenate(outcome_arr, on_dim)
+
+
+define_routes_all_for = functools.partial(_measure_local_data, on_dim=0)
 
 
 def partner_2(value, axis, stride):
@@ -55,7 +66,7 @@
     )
     partial_sum = jnp.dot(samples, local_rows, preferred_element_type=jnp.float32)
     sketched = lax.psum(partial_sum.astype(jnp.bfloat16), "col")
-    all_sketched = lax.all_gather(sketched, "row", axis=0, tiled=True)
+    all_sketched = define_routes_all_for(sketched)
     off_samples = off_products(all_sketched, front_blocks, block_cols, leaf_ids, top_level)
     leaf_basis = jax.vmap(cholqr)(off_samples[:, 0].astype(jnp.float32))
     carried = jnp.einsum(

time: 972 us -> 1230 us (1.27)
  waiting for transfers between devices: 215 us -> 478 us
  local copies, waits for them, and re-layouts: 101 us -> 86.4 us
    all_to_all x0 -> x1, waiting for transfers between devices: none -> 363 us  [_measure_local_data(): lax.all_to_all(jnp.stack([state for _ in range(lax.axis_size('row'))]), '...]
    all_gather x1 -> x0, waiting for transfers between devices: 98 us -> none  [shards(): all_sketched = lax.all_gather(sketched, 'row', axis=0, tiled=True)]
    reshape x1 -> x0, local copies, waits for them, and re-layouts: 22.4 us -> none  [off_products(): all_sketched.reshape(leaf_total, front_blocks.shape[2], all_sketched.shap...]
where the time goes in v1:
time: 1230 us; the launch traced here: 1220 us
  other arithmetic  563 us (46%)
  waiting for transfers between devices  478 us (39%)
  local copies, waits for them, and re-layouts  86.4 us (7%)
  matrix products  60.2 us (5%)
  between operations  20.7 us (2%)
  starting transfers between devices  13.2 us (1%)
    all_to_all x1, waiting for transfers between devices, _measure_local_data(): lax.all_to_all(jnp.stack([state for _ in range(lax.axis_size('row'))]), '...  363 us
    another operation x45, other arithmetic, cholqr(): low_factor = jnp.linalg.cholesky(gram_matrix)  359 us
    another operation x14, other arithmetic, cholqr(): jax.scipy.linalg.solve_triangular(low_factor, identity, lower=True)  201 us
    psum x1, waiting for transfers between devices, shards(): sketched = lax.psum(partial_sum.astype(jnp.bfloat16), 'col')  101 us
  transfers between devices with their start and end apart: 5, of which 5 were waited for; matrix products, arithmetic and copies ran while one was open for 0% of the time, Pallas kernels for 0%

profile of v1, /device:TPU:1, one launch (start us, length us, event | category | flops | bytes accessed | tf_op | source)
XLA Modules:
  0.0 1222.4 jit_solution(9506933671621273931)
XLA Ops:
  8.2 2.4 fusion.2
  10.6 100.7 %all-reduce.5.cloned.1.call-done = bf16[2048,256]{0,1:T(8,128)(2,1)} async-done(((bf16[2048,256]{0,1:T(8,128)(2,1)}), bf16[2048,256]{0,1:T(8,128)(2,1)}) %all-reduce.5.cloned.1.call-update) | async-done | bytes 1048592 | tf_op jit(solution)/shard_map/psum | solution.py:68
  112.8 5.9 stack.2
  118.8 9.3 all-to-all-start
  128.5 362.8 %all-to-all-done = bf16[16,2048,256]{2,1,0:T(8,128)(2,1)} async-done(((bf16[16,2048,256]{2,1,0:T(8,128)(2,1)}), bf16[16,2048,256]{2,1,0:T(8,128)(2,1)}, u32[]{:S(2)}, u32[]{:S(2)}) %all-to-all-start) | async-done | bytes 16777248 | tf_op jit(solution)/shard_map/all_to_all | solution.py:10
  491.3 9.9 gather_fusion
  501.3 12.5 %convolution_bitcast_fusion = f32[4,5,512,256]{2,3,1,0:T(8,128)} fusion(bf16[4,5,512,256]{3,2,1,0:T(8,128)(2,1)} %bitcast.432, bf16[4,5,512,512]{3,2,1,0:T(8,128)(2,1)} %param.7), kind=kOutput, calls=%fused_computation.17 | convolution fusion | flops 2684354560 | bytes 26214400 | tf_op jit(solution)/shard_map/nkab,nkbc->nkac/dot_general | solution.py:40
  513.8 17.1 %copy.96 = f32[4,5,512,256]{3,1,2,0:T(8,128)} copy(f32[4,5,512,256]{2,3,1,0:T(8,128)} %convolution_bitcast_fusion) | data formatting | bytes 20971520 | tf_op jit(solution)/shard_map/nkab,nkbc->nkac/dot_general | solution.py:40
  530.9 11.9 convolution_convert_fusion
  542.8 3.2 copy-done.2
  547.5 9.4 slice.235
  558.9 46.9 %custom-call.47 = f32[4,128,128]{2,1,0:T(8,128)S(1)} custom-call(f32[4,128,128]{2,1,0:T(8,128)S(1)} %cholesky.577), custom_call_target="Cholesky" | custom-call | tf_op jit(solution)/shard_map/vmap(jit(cholesky))/cholesky | solution.py:28
  605.9 39.3 %custom-call.48 = f32[4,1,128,128]{2,3,1,0:T(8,128)S(1)} custom-call(f32[4,1,128,128]{3,2,1,0:T(8,128)S(1)} %select_bitcast_fusion), custom_call_target="InvertDiagBlocksLowerTriangular" | custom-call | tf_op jit(solution)/shard_map/vmap(jit(cholesky))/cholesky | solution.py:28
  648.3 59.6 %custom-call.49 = f32[4,128,128]{2,1,0:T(8,128)S(1)} custom-call(f32[4,128,128]{2,1,0:T(8,128)S(1)} %convolution_subtract_fusion.2), custom_call_target="Cholesky" | custom-call | tf_op jit(solution)/shard_map/vmap(jit(cholesky))/cholesky | solution.py:28
  708.4 5.3 while.10
  713.7 79.4 %custom-call.50 = f32[4,2,128,128]{2,3,1,0:T(8,128)S(1)} custom-call(f32[4,2,128,128]{3,2,1,0:T(8,128)} %bitcast.450), custom_call_target="InvertDiagBlocksLowerTriangular" | custom-call | tf_op jit(solution)/shard_map/vmap(jit(_solve_triangular))/triangular_solve | solution.py:30
  795.1 2.7 multiply_convert_fusion.2
  797.8 5.7 multiply_convert_fusion
  809.9 24.3 %custom-call.51 = f32[2,128,128]{2,1,0:T(8,128)S(1)} custom-call(f32[2,128,128]{2,1,0:T(8,128)} %cholesky.580), custom_call_target="Cholesky" | custom-call | tf_op jit(solution)/shard_map/vmap(jit(cholesky))/cholesky | solution.py:28
  836.4 21.5 %custom-call.52 = f32[2,1,128,128]{2,3,1,0:T(8,128)} custom-call(f32[2,1,128,128]{3,2,1,0:T(8,128)} %select_bitcast_fusion.1), custom_call_target="InvertDiagBlocksLowerTriangular" | custom-call | tf_op jit(solution)/shard_map/vmap(jit(cholesky))/cholesky | solution.py:28
  861.7 24.9 %custom-call.53 = f32[2,128,128]{2,1,0:T(8,128)} custom-call(f32[2,128,128]{2,1,0:T(8,128)} %convolution_subtract_fusion.3), custom_call_target="Cholesky" | custom-call | tf_op jit(solution)/shard_map/vmap(jit(cholesky))/cholesky | solution.py:28
  890.5 8.3 while.11
  891.7 3.0 bitcast_dynamic-update-slice_fusion.17
  895.9 2.9 bitcast_dynamic-update-slice_fusion.17
  898.8 40.9 %custom-call.54 = f32[2,2,128,128]{2,3,1,0:T(8,128)} custom-call(f32[2,2,128,128]{3,2,1,0:T(8,128)} %bitcast.451), custom_call_target="InvertDiagBlocksLowerTriangular" | custom-call | tf_op jit(solution)/shard_map/vmap(jit(_solve_triangular))/triangular_solve | solution.py:30
  945.8 11.7 custom-call.67
  957.6 9.8 custom-call.68
  967.9 12.1 custom-call.69
  982.8 4.1 while.12
  986.9 19.7 %custom-call.70 = f32[1,2,128,128]{2,3,1,0:T(8,128)S(1)} custom-call(f32[1,2,128,128]{3,2,1,0:T(8,128)S(1)} %bitcast.447), custom_call_target="InvertDiagBlocksLowerTriangular" | custom-call | tf_op jit(solution)/shard_map/vmap(jit(_solve_triangular))/triangular_solve | solution.py:30
  1011.2 11.7 custom-call.71
  1022.9 9.8 custom-call.72
  1033.2 11.7 custom-call.73
  1047.6 4.2 while.13
  1051.9 19.7 %custom-call.74 = f32[1,2,128,128]{2,3,1,0:T(8,128)S(1)} custom-call(f32[1,2,128,128]{3,2,1,0:T(8,128)S(1)} %bitcast.448), custom_call_target="InvertDiagBlocksLowerTriangular" | custom-call | tf_op jit(solution)/shard_map/vmap(jit(_solve_triangular))/triangular_solve | solution.py:30
  1074.0 6.9 collective-permute-done.1
  1081.4 11.7 custom-call.75
  1093.1 9.8 custom-call.76
  1103.4 11.7 custom-call.77
  1117.8 4.3 while.14
  1122.1 19.7 %custom-call.78 = f32[1,2,128,128]{2,3,1,0:T(8,128)S(1)} custom-call(f32[1,2,128,128]{3,2,1,0:T(8,128)S(1)} %bitcast.449), custom_call_target="InvertDiagBlocksLowerTriangular" | custom-call | tf_op jit(solution)/shard_map/vmap(jit(_solve_triangular))/triangular_solve | solution.py:30
  1143.4 2.2 collective-permute-start.2
  1145.6 6.4 collective-permute-done.2
  1152.5 11.7 custom-call.79
  1164.3 9.8 custom-call.80
  1174.6 11.7 custom-call.81
  1189.1 4.4 while.15
  1193.5 19.7 %custom-call.82 = f32[1,2,128,128]{2,3,1,0:T(8,128)S(1)} custom-call(f32[1,2,128,128]{3,2,1,0:T(8,128)S(1)} %bitcast.446), custom_call_target="InvertDiagBlocksLowerTriangular" | custom-call | tf_op jit(solution)/shard_map/vmap(jit(_solve_triangular))/triangular_solve | solution.py:30
  (199 shorter events, 77.0 us)
Async XLA Ops:
  7.2 1.1 copy-start
  7.2 104.2 %all-reduce.5.cloned.1.call-start = ((), (), s32[]{:S(2)}) async-start(), calls=%async_computation.1 | async-start | bytes 2097152 | tf_op jit(solution)/shard_map/psum | solution.py:68
  118.7 9.4 copy-start.11
  118.8 372.6 %all-to-all-start = ((bf16[16,2048,256]{2,1,0:T(8,128)(2,1)}), bf16[16,2048,256]{2,1,0:T(8,128)(2,1)}, u32[]{:S(2)}, u32[]{:S(2)}) async-start(bf16[16,2048,256]{2,1,0:T(8,128)(2,1)} %stack.2), calls=%async_computation | async-start | bytes 33554432 | tf_op jit(solution)/shard_map/all_to_all | solution.py:10
  128.2 477.6 %copy-start.10 = (pred[128,128]{1,0:T(8,128)(4,1)}, pred[128,128]{1,0:T(8,128)(4,1)S(1)}, u32[]{:S(2)}) copy-start(pred[128,128]{1,0:T(8,128)(4,1)S(1)} %iota_compare_fusion.5) | copy-start | bytes 49156
  128.3 579.8 %copy-start.9 = (pred[256,256]{1,0:T(8,128)(4,1)}, pred[256,256]{1,0:T(8,128)(4,1)S(1)}, u32[]{:S(2)}) copy-start(pred[256,256]{1,0:T(8,128)(4,1)S(1)} %iota_compare_fusion.2) | copy-start | bytes 196612
  128.5 664.7 %copy-start.6 = (f32[128,256]{1,0:T(8,128)}, f32[128,256]{1,0:T(8,128)S(1)}, u32[]{:S(2)}) copy-start(f32[128,256]{1,0:T(8,128)S(1)} %get-tuple-element.125) | copy-start | bytes 393220
  128.5 665.3 %copy-start.8 = (f32[128,256]{1,0:T(8,128)}, f32[128,256]{1,0:T(8,128)S(1)}, u32[]{:S(2)}) copy-start(f32[128,256]{1,0:T(8,128)S(1)} %get-tuple-element.124) | copy-start | bytes 393220
  542.8 3.2 copy-start.2
  547.5 9.4 copy-start.4
  558.0 1.0 copy-start.3
  713.7 84.0 %copy-start.13 = (s32[2,2]{1,0:T(2,128)}, s32[2,2]{1,0:T(2,128)S(1)}, u32[]{:S(2)}) copy-start(s32[2,2]{1,0:T(2,128)S(1)} %get-tuple-element.440) | copy-start | bytes 52
  797.7 5.7 copy-start.12
  808.4 0.8 copy-start.5
  888.2 51.5 %copy-start.7 = (f32[128,256]{1,0:T(8,128)S(1)}, f32[128,256]{1,0:T(8,128)}, u32[]{:S(2)}) copy-start(f32[128,256]{1,0:T(8,128)} %copy-done.6) | copy-start | bytes 393220
  945.3 37.5 %copy-start.14 = (s32[2,2]{1,0:T(2,128)S(1)}, s32[2,2]{1,0:T(2,128)}, u32[]{:S(2)}) copy-start(s32[2,2]{1,0:T(2,128)} %get-tuple-element.441) | copy-start | bytes 52
  1008.3 2.3 collective-permute-start
  1073.3 7.6 collective-permute-start.1
  1143.4 8.6 collective-permute-start.2
  1152.4 62.7 %copy-start.1 = (bf16[1024,256]{1,0:T(8,128)(2,1)S(1)}, bf16[1024,256]{1,0:T(8,128)(2,1)}, u32[]{:S(2)}) copy-start(bf16[1024,256]{1,0:T(8,128)(2,1)} %param.10) | copy-start | bytes 1572868
Sparse Core Ops, SparseCore 0:
  11.8 99.4 all-reduce.4
